TPU v7x, 128 devices: a whole 4x4x4 slice. The times are simulated.
128 devices in a mesh: row: 8 (over y, core), col: 16 (over x, z).
Axes of the slice: x: 4, y: 4, z: 4, core: 2. Of those that a mesh axis runs over, the one named last changes fastest.
Arguments:
- tokens: bfloat16 [2048, 8192], P('col', 'row'), may hold values from -6 to 6
- gate_weight: bfloat16 [8192, 28672], P('row', 'col'), may hold values from -0.109375 to 0.109375
- up_weight: bfloat16 [8192, 28672], P('row', 'col'), may hold values from -0.109375 to 0.109375
- down_weight: bfloat16 [28672, 8192], P('col', 'row'), may hold values from -0.0546875 to 0.0546875
- gate_keep: int32 [224, 48], P('col'), may hold values from 0 to 63, as said below
- gate_count: int32 [224], P('col'), may hold values from 5 to 48, as said below
- up_keep: int32 [224, 48], P('col'), may hold values from 0 to 63, as said below
- up_count: int32 [224], P('col'), may hold values from 5 to 48, as said below
- down_keep: int32 [64, 176], P('row'), may hold values from 0 to 223, as said below
- down_count: int32 [64], P('row'), may hold values from 15 to 176, as said below
Outputs:
- output_rows: bfloat16 [2048, 8192], P('col', 'row')
Inputs may be any that keep to these rules, and one draw needn't show every extreme that they name: `gate_keep`: each row holds distinct block indices of the model features. `gate_count`: some block column uses all 48 slots. `up_keep`: each row holds distinct block indices of the model features. `up_count`: some block column uses all 48 slots. `down_keep`: each row holds distinct block indices of the hidden units. `down_count`: some block column uses all 176 slots.
All inputs are finite; a program needn't handle non-finite values.
Results may differ from a plain program's by a relative error of at most 0.028.
Values may be sent and summed in bfloat16 or wider, within the bound.
A program may use at most 128 MiB of HBM per device.

v0:
```python
import jax
import jax.numpy as jnp
from jax import lax
from jax.sharding import PartitionSpec as P

BLOCK = 128
CHUNKS = 1
COL_A2A = True
COL_RING = False


def local_mask(keep_list, keep_count, offset, blocks):
    position = jnp.arange(keep_list.shape[1], dtype=jnp.int32)
    active_slot = position[None, :] < keep_count[:, None]
    local_index = keep_list - offset
    matches = (
        local_index[:, :, None] == jnp.arange(blocks, dtype=jnp.int32)[None, None, :]
    ) & active_slot[:, :, None]
    return jnp.any(matches, axis=1)


def apply_mask(weight, block_mask, block_size):
    block_rows, block_cols = block_mask.shape
    shaped = weight.reshape(block_rows, block_size, block_cols, block_size)
    masked = jnp.where(block_mask[:, None, :, None], shaped, jnp.zeros((), weight.dtype))
    return masked.reshape(weight.shape)


def row_perm(n_row, step):
    n_y = n_row // 2
    return [(y * 2 + c, (y + step) % n_y * 2 + c) for y in range(n_y) for c in range(2)]


def row_reduce_scatter(tokens, weights, n_row, after):
    n_y = n_row // 2
    r = lax.axis_index("row")
    y = r // 2
    core = r % 2
    rows = tokens.shape[0]
    width = weights.shape[1]
    halves = tokens.reshape(2, rows // 2, tokens.shape[1])
    send = lax.dynamic_index_in_dim(halves, 1 - core, 0, keepdims=False)
    keep = lax.dynamic_index_in_dim(halves, core, 0, keepdims=False)
    send = jnp.dot(send, weights, preferred_element_type=jnp.float32).astype(jnp.bfloat16)
    swap = [(i, i ^ 1) for i in range(n_row)]
    got = lax.ppermute(send, "row", swap)
    keep = jnp.dot(keep, weights, preferred_element_type=jnp.float32).astype(jnp.bfloat16)
    pair = (keep.astype(jnp.float32) + got.astype(jnp.float32)).astype(jnp.bfloat16)
    if after is not None:
        pair, after = lax.optimization_barrier((pair, after))
    chunk = rows // 2 // n_y
    pair = pair.reshape(n_y, chunk, width)
    results = []
    for direction, cols in ((1, slice(0, width // 2)), (-1, slice(width // 2, width))):
        own = pair[:, :, cols]
        index = (y - direction) % n_y
        acc = lax.dynamic_index_in_dim(own, index, 0, keepdims=False)
        for step in range(n_y - 1):
            got = lax.ppermute(acc.astype(jnp.bfloat16), "row", row_perm(n_row, direction))
            index = (index - direction) % n_y
            acc = got.astype(jnp.float32) + lax.dynamic_index_in_dim(own, index, 0, keepdims=False)
        results.append(acc)
    return results


def row_all_gather(value, n_row):
    n_y = n_row // 2
    r = lax.axis_index("row")
    y = r // 2
    core = r % 2
    chunk, width = value.shape
    parts = []
    for direction, cols in ((1, slice(0, width // 2)), (-1, slice(width // 2, width))):
        held = value[:, cols]
        full = jnp.zeros((n_y, chunk, width // 2), value.dtype)
        full = lax.dynamic_update_index_in_dim(full, held, y, 0)
        for step in range(n_y - 1):
            held = lax.ppermute(held, "row", row_perm(n_row, direction))
            full = lax.dynamic_update_index_in_dim(
                full, held, (y - direction * (step + 1)) % n_y, 0
            )
        parts.append(full)
    half = jnp.concatenate(parts, axis=2).reshape(n_y * chunk, width)
    swap = [(i, i ^ 1) for i in range(n_row)]
    other = lax.ppermute(half, "row", swap)
    both = jnp.zeros((2, n_y * chunk, width), value.dtype)
    both = lax.dynamic_update_index_in_dim(both, half, core, 0)
    both = lax.dynamic_update_index_in_dim(both, other, 1 - core, 0)
    return both.reshape(2 * n_y * chunk, width)


def ring_reduce_scatter(own, pos, n, perm_of):
    width = own.shape[2]
    halves = []
    for direction, cols in ((1, slice(0, width // 2)), (-1, slice(width // 2, width))):
        part = own[:, :, cols]
        index = (pos - direction) % n
        acc = lax.dynamic_index_in_dim(part, index, 0, keepdims=False).astype(jnp.float32)
        for step in range(n - 1):
            got = lax.ppermute(acc.astype(jnp.bfloat16), "col", perm_of(direction))
            index = (index - direction) % n
            acc = got.astype(jnp.float32) + lax.dynamic_index_in_dim(part, index, 0, keepdims=False)
        halves.append(acc)
    return jnp.concatenate(halves, axis=1)


def ring_all_gather(value, pos, n, perm_of):
    chunk, width = value.shape
    parts = []
    for direction, cols in ((1, slice(0, width // 2)), (-1, slice(width // 2, width))):
        held = value[:, cols]
        full = jnp.zeros((n, chunk, width // 2), value.dtype)
        full = lax.dynamic_update_index_in_dim(full, held, pos, 0)
        for step in range(n - 1):
            held = lax.ppermute(held, "col", perm_of(direction))
            full = lax.dynamic_update_index_in_dim(
                full, held, (pos - direction * (step + 1)) % n, 0
            )
        parts.append(full)
    return jnp.concatenate(parts, axis=2)


def col_axes(n_col):
    n_z = 4 if n_col % 4 == 0 else 1
    n_x = n_col // n_z
    c = lax.axis_index("col")

    def x_perm(d):
        return [(i * n_z + j, (i + d) % n_x * n_z + j) for i in range(n_x) for j in range(n_z)]

    def z_perm(d):
        return [(i * n_z + j, i * n_z + (j + d) % n_z) for i in range(n_x) for j in range(n_z)]

    return (n_x, n_z, c // n_z, c % n_z, x_perm, z_perm)


def col_all_gather(value, n_col):
    n_x, n_z, x, z, x_perm, z_perm = col_axes(n_col)
    rows, width = value.shape
    part = ring_all_gather(value, z, n_z, z_perm).reshape(n_z * rows, width)
    return ring_all_gather(part, x, n_x, x_perm).reshape(n_x * n_z * rows, width)


def col_reduce_scatter(terms, n_col):
    n_z = 4 if n_col % 4 == 0 else 1
    n_x = n_col // n_z
    c = lax.axis_index("col")
    x = c // n_z
    z = c % n_z
    rows, width = terms.shape

    def x_perm(d):
        return [(i * n_z + j, (i + d) % n_x * n_z + j) for i in range(n_x) for j in range(n_z)]

    def z_perm(d):
        return [(i * n_z + j, i * n_z + (j + d) % n_z) for i in range(n_x) for j in range(n_z)]

    part = ring_reduce_scatter(terms.reshape(n_x, rows // n_x, width), x, n_x, x_perm)
    part = part.astype(jnp.bfloat16).reshape(n_z, rows // n_x // n_z, width)
    return ring_reduce_scatter(part, z, n_z, z_perm).astype(jnp.bfloat16)


def on_device(
    tokens,
    gate_weight,
    up_weight,
    down_weight,
    gate_keep,
    gate_count,
    up_keep,
    up_count,
    down_keep,
    down_count,
):
    model_blocks = gate_weight.shape[0] // BLOCK
    hidden_blocks = gate_weight.shape[1] // BLOCK
    n_col = lax.axis_size("col")
    n_row = lax.axis_size("row")
    row_offset = lax.axis_index("row") * model_blocks
    col_offset = lax.axis_index("col") * hidden_blocks
    gate_pruned = apply_mask(
        gate_weight, local_mask(gate_keep, gate_count, row_offset, model_blocks).T, BLOCK
    )
    up_pruned = apply_mask(
        up_weight, local_mask(up_keep, up_count, row_offset, model_blocks).T, BLOCK
    )
    down_pruned = apply_mask(
        down_weight, local_mask(down_keep, down_count, col_offset, hidden_blocks).T, BLOCK
    )
    both_weights = jnp.concatenate([gate_pruned, up_pruned], axis=1)
    rows = tokens.shape[0] // CHUNKS
    gathered = lax.all_gather(tokens, "col", axis=0, tiled=True)
    gathered = gathered.reshape(n_col, CHUNKS, rows, gathered.shape[1])
    outs = []
    previous = None
    for k in range(CHUNKS):
        chunk = gathered[:, k].reshape(n_col * rows, gathered.shape[3])
        gate_sums, up_sums = row_reduce_scatter(chunk, both_weights, n_row, previous)
        hidden = (jax.nn.silu(gate_sums) * up_sums).astype(jnp.bfloat16)
        hidden = row_all_gather(hidden, n_row)
        terms = jnp.dot(hidden, down_pruned, preferred_element_type=jnp.float32).astype(
            jnp.bfloat16
        )
        previous = terms
        if COL_RING:
            outs.append(col_reduce_scatter(terms, n_col))
        elif COL_A2A and k == CHUNKS - 1:
            split = terms.shape[1] // 2
            left = lax.psum_scatter(terms[:, :split], "col", scatter_dimension=0, tiled=True)
            right = terms[:, split:].reshape(n_col, rows, terms.shape[1] - split)
            right = lax.all_to_all(right, "col", 0, 0, tiled=False)
            right = jnp.sum(right.astype(jnp.float32), axis=0).astype(jnp.bfloat16)
            outs.append(jnp.concatenate([left, right], axis=1))
        else:
            outs.append(lax.psum_scatter(terms, "col", scatter_dimension=0, tiled=True))
    return jnp.concatenate(outs, axis=0)


def solution(mesh):
    return jax.shard_map(
        on_device,
        mesh=mesh,
        in_specs=(
            P("col", "row"),
            P("row", "col"),
            P("row", "col"),
            P("col", "row"),
            P("col", None),
            P("col"),
            P("col", None),
            P("col"),
            P("row", None),
            P("row"),
        ),
        out_specs=P("col", "row"),
        check_vma=False,
    )
```

profile of v0, /device:TPU:0, one launch (start us, length us, event | category | flops | bytes accessed | tf_op | source)
XLA Modules:
  0.0 336.2 jit_solution(16218142034892544650)
XLA Ops:
  6.5 0.7 all-gather.2.cloned.1.call-update
  7.3 6.0 %copy.14 = bf16[1024,1792]{0,1:T(8,128)(2,1)} copy(bf16[1024,1792]{1,0:T(8,128)(2,1)} %param.12) | data formatting | bytes 7340032 | tf_op args[2]
  13.3 6.0 %copy.13 = bf16[1024,1792]{0,1:T(8,128)(2,1)} copy(bf16[1024,1792]{1,0:T(8,128)(2,1)} %param.11) | data formatting | bytes 7340032 | tf_op args[1]
  19.3 0.1 iota_compare_fusion.4
  19.4 0.3 fusion.16
  19.7 0.1 iota_compare_fusion.5
  19.8 0.3 fusion.14
  20.1 0.5 broadcast_in_dim.93
  20.7 5.1 %bitcast_select_fusion.1 = bf16[1024,1792]{0,1:T(8,128)(2,1)} fusion(bf16[1024,1792]{0,1:T(8,128)(2,1)} %copy.14, pred[224,8,8,128]{3,2,1,0:T(8,128)(4,1)S(1)} %bitcast.78), kind=kLoop, calls=%fused_computation.5 | loop fusion | flops 1835008 | bytes 9175040 | tf_op jit(solution)/shard_map/jit(_where)/select_n | solution.py:25
  25.8 0.5 broadcast_in_dim.90
  26.4 2.8 bitcast_select_fusion.2
  29.2 34.3 %all-gather.2.cloned.1.call-done = bf16[2048,1024]{1,0:T(8,128)(2,1)} async-done(((bf16[128,1024]{1,0:T(8,128)(2,1)}), bf16[2048,1024]{1,0:T(8,128)(2,1)}) %all-gather.2.cloned.1.call-update) | async-done | bytes 4194320 | tf_op jit(solution)/shard_map/all_gather | solution.py:192
  63.5 13.4 %convolution_convert_fusion = bf16[1024,3584]{1,0:T(8,128)(2,1)} fusion(bf16[1024,1792]{0,1:T(8,128)(2,1)} %bitcast_select_fusion.1, bf16[1024,1792]{0,1:T(8,128)(2,1)} %bitcast_select_fusion.2, bf16[2,1024,1024]{2,1,0:T(8,128)(2,1)} %bitcast.84, s32[]{:T(128)S(6)} %select_n.138), kind=kOutput, calls=%fused_computation.1 | convolution fusion | flops 7534542848 | bytes 16777220 | tf_op jit(solution)/shard_map/dot_general | solution.py:44
  76.9 12.0 %collective-permute-done = bf16[1024,3584]{1,0:T(8,128)(2,1)} collective-permute-done((bf16[1024,3584]{1,0:T(8,128)(2,1)}, bf16[1024,3584]{1,0:T(8,128)(2,1)}, u32[]{:S(2)}, u32[]{:S(2)}) %collective-permute-start) | collective-permute-done | bytes 7340064 | tf_op jit(solution)/shard_map/ppermute | solution.py:46
  88.9 14.5 %add_convert_fusion = bf16[1024,3584]{1,0:T(8,128)(2,1)} fusion(bf16[1024,3584]{1,0:T(8,128)(2,1)} %collective-permute-done, bf16[1024,1792]{0,1:T(8,128)(2,1)} %bitcast_select_fusion.1, bf16[1024,1792]{0,1:T(8,128)(2,1)} %bitcast_select_fusion.2, bf16[2,1024,1024]{2,1,0:T(8,128)(2,1)} %bitcast.85, s32[]{:T(128)S(6)} %select_n.135), kind=kOutput, calls=%fused_computation | convolution fusion | flops 7549222912 | bytes 24117252 | tf_op jit(solution)/shard_map/dot_general | solution.py:47
  103.4 5.4 %fusion.22 = (bf16[4,256,1792]{2,1,0:T(8,128)(2,1)S(1)}, bf16[4,256,1792]{2,1,0:T(8,128)(2,1)}) fusion(bf16[4,256,3584]{2,1,0:T(8,128)(2,1)} %bitcast.76), kind=kLoop, calls=%fused_computation.59 | loop fusion | bytes 14680064 | tf_op jit(solution)/shard_map/slice | solution.py:55
  108.8 1.8 copy-done
  110.7 0.1 dynamic-slice_bitcast_fusion.1
  110.7 1.6 collective-permute-start.1
  112.3 2.2 dynamic-slice_bitcast_fusion
  114.5 1.8 collective-permute-start.4
  116.2 18.1 %collective-permute-done.1 = bf16[256,1792]{1,0:T(8,128)(2,1)S(1)} collective-permute-done((bf16[256,1792]{1,0:T(8,128)(2,1)S(1)}, bf16[256,1792]{1,0:T(8,128)(2,1)S(1)}, u32[]{:S(2)}, u32[]{:S(2)}) %collective-permute-start.1) | collective-permute-done | bytes 917536 | tf_op jit(solution)/shard_map/ppermute | solution.py:59
  134.4 1.4 fusion.9
  135.8 0.3 collective-permute-start.2
  136.1 0.7 collective-permute-done.4
  136.8 2.4 fusion.7
  139.2 3.0 collective-permute-start.5
  142.2 16.4 %collective-permute-done.2 = bf16[256,1792]{1,0:T(8,128)(2,1)S(1)} collective-permute-done((bf16[256,1792]{1,0:T(8,128)(2,1)S(1)}, bf16[256,1792]{1,0:T(8,128)(2,1)S(1)}, u32[]{:S(2)}, u32[]{:S(2)}) %collective-permute-start.2) | collective-permute-done | bytes 917536 | tf_op jit(solution)/shard_map/ppermute | solution.py:59
  158.6 1.4 fusion.8
  160.0 0.1 collective-permute-start.3
  160.1 1.2 collective-permute-done.5
  161.3 2.7 fusion.6
  163.9 3.7 %collective-permute-start.6 = (bf16[256,1792]{1,0:T(8,128)(2,1)}, bf16[256,1792]{1,0:T(8,128)(2,1)S(1)}, u32[]{:S(2)}, u32[]{:S(2)}) collective-permute-start(bf16[256,1792]{1,0:T(8,128)(2,1)} %fusion.6), channel_id=1, source_target_pairs={{0,96},{16,112},{32,0},{48,16},{64,32},{80,48},{96,64},{112,80},{1... | collective-permute-start | bytes 2752520 | tf_op jit(solution)/shard_map/ppermute | solution.py:59
  167.6 14.3 %collective-permute-done.3 = bf16[256,1792]{1,0:T(8,128)(2,1)S(1)} collective-permute-done((bf16[256,1792]{1,0:T(8,128)(2,1)S(1)}, bf16[256,1792]{1,0:T(8,128)(2,1)S(1)}, u32[]{:S(2)}, u32[]{:S(2)}) %collective-permute-start.3) | collective-permute-done | bytes 917536 | tf_op jit(solution)/shard_map/ppermute | solution.py:59
  181.9 3.9 %collective-permute-done.6 = bf16[256,1792]{1,0:T(8,128)(2,1)S(1)} collective-permute-done((bf16[256,1792]{1,0:T(8,128)(2,1)}, bf16[256,1792]{1,0:T(8,128)(2,1)S(1)}, u32[]{:S(2)}, u32[]{:S(2)}) %collective-permute-start.6) | collective-permute-done | bytes 917536 | tf_op jit(solution)/shard_map/ppermute | solution.py:59
  185.9 2.2 fusion.5
  188.1 0.1 fusion.24
  188.1 0.1 collective-permute-start.7
  188.2 3.7 %collective-permute-start.10 = (bf16[256,896]{1,0:T(8,128)(2,1)S(1)}, bf16[256,896]{1,0:T(8,128)(2,1)S(1)}, u32[]{:S(2)}, u32[]{:S(2)}) collective-permute-start(bf16[256,896]{1,0:T(8,128)(2,1)S(1)} %get-tuple-element.10), channel_id=1, source_target_pairs={{0,96},{16,112},{32,0},{48,16},{64,32},{80,48},{96,64},{112,80},{1... | collective-permute-start | bytes 1376264 | tf_op jit(solution)/shard_map/ppermute | solution.py:78
  191.9 0.1 broadcast.73.clone.1
  192.0 0.1 bitcast_dynamic-update-slice_fusion.9
  192.1 0.1 broadcast.73.clone
  192.2 0.1 bitcast_dynamic-update-slice_fusion.5
  192.3 7.5 %collective-permute-done.7 = bf16[256,896]{1,0:T(8,128)(2,1)S(1)} collective-permute-done((bf16[256,896]{1,0:T(8,128)(2,1)S(1)}, bf16[256,896]{1,0:T(8,128)(2,1)S(1)}, u32[]{:S(2)}, u32[]{:S(2)}) %collective-permute-start.7) | collective-permute-done | bytes 458784 | tf_op jit(solution)/shard_map/ppermute | solution.py:78
  199.8 3.2 collective-permute-start.11
  203.1 7.3 %collective-permute-done.8 = bf16[256,896]{1,0:T(8,128)(2,1)S(1)} collective-permute-done((bf16[256,896]{1,0:T(8,128)(2,1)S(1)}, bf16[256,896]{1,0:T(8,128)(2,1)S(1)}, u32[]{:S(2)}, u32[]{:S(2)}) %collective-permute-start.8) | collective-permute-done | bytes 458784 | tf_op jit(solution)/shard_map/ppermute | solution.py:78
  210.5 3.2 collective-permute-start.12
  213.8 0.1 bitcast_dynamic-update-slice_fusion.3
  213.8 6.3 %collective-permute-done.9 = bf16[256,896]{1,0:T(8,128)(2,1)S(1)} collective-permute-done((bf16[256,896]{1,0:T(8,128)(2,1)S(1)}, bf16[256,896]{1,0:T(8,128)(2,1)S(1)}, u32[]{:S(2)}, u32[]{:S(2)}) %collective-permute-start.9) | collective-permute-done | bytes 458784 | tf_op jit(solution)/shard_map/ppermute | solution.py:78
  220.2 0.1 bitcast_dynamic-update-slice_fusion.2
  220.3 2.0 pad_maximum_fusion.3
  222.4 0.1 iota_compare_fusion.3
  222.4 0.3 fusion.12
  222.8 0.5 broadcast_in_dim.89
  223.2 2.5 bitcast_dynamic-update-slice_fusion.1
  225.7 3.4 %collective-permute-done.13 = bf16[1024,1792]{1,0:T(8,128)(2,1)} collective-permute-done((bf16[1024,1792]{1,0:T(8,128)(2,1)}, bf16[1024,1792]{1,0:T(8,128)(2,1)}, u32[]{:S(2)}, u32[]{:S(2)}) %collective-permute-start.13) | collective-permute-done | bytes 3670048 | tf_op jit(solution)/shard_map/ppermute | solution.py:85
  229.1 2.5 bitcast_dynamic-update-slice_fusion
  231.6 0.5 broadcast_in_dim.105
  232.1 8.2 %convolution_convert_fusion.2 = bf16[2048,1024]{1,0:T(8,128)(2,1)S(1)} fusion(bf16[2048,1792]{1,0:T(8,128)(2,1)S(1)} %bitcast.77, bf16[1792,1024]{1,0:T(8,128)(2,1)S(1)} %copy-done.8, pred[224,8,8,128]{3,2,1,0:T(8,128)(4,1)S(1)} %bitcast.80), kind=kOutput, calls=%fused_computation.7 | convolution fusion | flops 7520124928 | bytes 17039360 | tf_op jit(solution)/shard_map/dot_general | solution.py:201
  240.4 2.3 fusion.23
  242.7 37.1 %all_to_all.5 = bf16[16,128,512]{2,1,0:T(8,128)(2,1)S(1)} all-to-all(bf16[16,128,512]{2,1,0:T(8,128)(2,1)} %bitcast.75), channel_id=1, replica_groups=mesh['row'=8,'col'=16] {'col'}, dimensions={0} | all-to-all | bytes 4194304 | tf_op jit(solution)/shard_map/all_to_all | solution.py:211
  279.8 0.3 reduce_sum.12
  280.1 47.7 %reduce-scatter.2.cloned.1.call-done = bf16[128,512]{1,0:T(8,128)(2,1)} async-done(((bf16[2048,512]{1,0:T(8,128)(2,1)}), bf16[128,512]{1,0:T(8,128)(2,1)}) %reduce-scatter.2.cloned.1.call-update) | async-done | bytes 131088 | tf_op jit(solution)/shard_map/reduce_scatter | solution.py:209
  327.7 1.6 pad_maximum_fusion.4
  (33 shorter events, 0.3 us)
Async XLA Ops:
  6.5 57.0 %all-gather.2.cloned.1.call-start = ((), (), s32[]{:S(2)}) async-start(), calls=%async_computation.2 | async-start | bytes 4456448 | tf_op jit(solution)/shard_map/all_gather | solution.py:192
  7.3 320.5 %reduce-scatter.2.cloned.1.call-start = ((), (), s32[]{:S(2)}) async-start(), calls=%async_computation.3 | async-start | bytes 2228224 | tf_op jit(solution)/shard_map/reduce_scatter | solution.py:209
  13.3 6.0 %copy-start.5 = (s32[14]{0:T(128)S(1)}, s32[14]{0:T(128)}, u32[]{:S(2)}) copy-start(s32[14]{0:T(128)} %param.17) | copy-start | bytes 172
  13.3 6.1 %copy-start.3 = (s32[14,48]{1,0:T(8,128)S(1)}, s32[14,48]{1,0:T(8,128)}, u32[]{:S(2)}) copy-start(s32[14,48]{1,0:T(8,128)} %param.16) | copy-start | bytes 8068
  13.3 6.1 %copy-start.4 = (s32[14,48]{1,0:T(8,128)S(1)}, s32[14,48]{1,0:T(8,128)}, u32[]{:S(2)}) copy-start(s32[14,48]{1,0:T(8,128)} %param.14) | copy-start | bytes 8068
  13.3 6.4 %copy-start.6 = (s32[14]{0:T(128)S(1)}, s32[14]{0:T(128)}, u32[]{:S(2)}) copy-start(s32[14]{0:T(128)} %param.15) | copy-start | bytes 172
  20.7 5.7 %copy-start.1 = (bf16[1024,1792]{0,1:T(8,128)(2,1)S(1)}, bf16[1024,1792]{0,1:T(8,128)(2,1)}, u32[]{:S(2)}) copy-start(bf16[1024,1792]{0,1:T(8,128)(2,1)} %copy.13) | copy-start | bytes 11010052
  76.9 12.0 %collective-permute-start = (bf16[1024,3584]{1,0:T(8,128)(2,1)}, bf16[1024,3584]{1,0:T(8,128)(2,1)}, u32[]{:S(2)}, u32[]{:S(2)}) collective-permute-start(bf16[1024,3584]{1,0:T(8,128)(2,1)} %convolution_convert_fusion), channel_id=1, source_target_pairs={{0,16},{16,0},{32,48},{48,32},{64,80},{80,64},{96,112},{112,96},{1... | collective-permute-start | bytes 22020104 | tf_op jit(solution)/shard_map/ppermute | solution.py:46
  108.8 1.8 copy-start
  110.7 23.7 %collective-permute-start.1 = (bf16[256,1792]{1,0:T(8,128)(2,1)S(1)}, bf16[256,1792]{1,0:T(8,128)(2,1)S(1)}, u32[]{:S(2)}, u32[]{:S(2)}) collective-permute-start(bf16[256,1792]{1,0:T(8,128)(2,1)S(1)} %dynamic-slice_bitcast_fusion.1), channel_id=1, source_target_pairs={{0,32},{16,48},{32,64},{48,80},{64,96},{80,112},{96,0},{112,16},{1... | collective-permute-start | bytes 2752520 | tf_op jit(solution)/shard_map/ppermute | solution.py:59
  114.5 22.3 %collective-permute-start.4 = (bf16[256,1792]{1,0:T(8,128)(2,1)}, bf16[256,1792]{1,0:T(8,128)(2,1)S(1)}, u32[]{:S(2)}, u32[]{:S(2)}) collective-permute-start(bf16[256,1792]{1,0:T(8,128)(2,1)} %dynamic-slice_bitcast_fusion), channel_id=1, source_target_pairs={{0,96},{16,112},{32,0},{48,16},{64,32},{80,48},{96,64},{112,80},{1... | collective-permute-start | bytes 2752520 | tf_op jit(solution)/shard_map/ppermute | solution.py:59
  135.8 22.8 %collective-permute-start.2 = (bf16[256,1792]{1,0:T(8,128)(2,1)S(1)}, bf16[256,1792]{1,0:T(8,128)(2,1)S(1)}, u32[]{:S(2)}, u32[]{:S(2)}) collective-permute-start(bf16[256,1792]{1,0:T(8,128)(2,1)S(1)} %fusion.9), channel_id=1, source_target_pairs={{0,32},{16,48},{32,64},{48,80},{64,96},{80,112},{96,0},{112,16},{1... | collective-permute-start | bytes 2752520 | tf_op jit(solution)/shard_map/ppermute | solution.py:59
  139.2 22.0 %collective-permute-start.5 = (bf16[256,1792]{1,0:T(8,128)(2,1)}, bf16[256,1792]{1,0:T(8,128)(2,1)}, u32[]{:S(2)}, u32[]{:S(2)}) collective-permute-start(bf16[256,1792]{1,0:T(8,128)(2,1)} %fusion.7), channel_id=1, source_target_pairs={{0,96},{16,112},{32,0},{48,16},{64,32},{80,48},{96,64},{112,80},{1... | collective-permute-start | bytes 2752520 | tf_op jit(solution)/shard_map/ppermute | solution.py:59
  160.0 22.0 %collective-permute-start.3 = (bf16[256,1792]{1,0:T(8,128)(2,1)S(1)}, bf16[256,1792]{1,0:T(8,128)(2,1)S(1)}, u32[]{:S(2)}, u32[]{:S(2)}) collective-permute-start(bf16[256,1792]{1,0:T(8,128)(2,1)S(1)} %fusion.8), channel_id=1, source_target_pairs={{0,32},{16,48},{32,64},{48,80},{64,96},{80,112},{96,0},{112,16},{1... | collective-permute-start | bytes 2752520 | tf_op jit(solution)/shard_map/ppermute | solution.py:59
  163.9 21.9 %collective-permute-start.6 = (bf16[256,1792]{1,0:T(8,128)(2,1)}, bf16[256,1792]{1,0:T(8,128)(2,1)S(1)}, u32[]{:S(2)}, u32[]{:S(2)}) collective-permute-start(bf16[256,1792]{1,0:T(8,128)(2,1)} %fusion.6), channel_id=1, source_target_pairs={{0,96},{16,112},{32,0},{48,16},{64,32},{80,48},{96,64},{112,80},{1... | collective-permute-start | bytes 2752520 | tf_op jit(solution)/shard_map/ppermute | solution.py:59
  188.1 11.6 %collective-permute-start.7 = (bf16[256,896]{1,0:T(8,128)(2,1)S(1)}, bf16[256,896]{1,0:T(8,128)(2,1)S(1)}, u32[]{:S(2)}, u32[]{:S(2)}) collective-permute-start(bf16[256,896]{1,0:T(8,128)(2,1)S(1)} %get-tuple-element.9), channel_id=1, source_target_pairs={{0,32},{16,48},{32,64},{48,80},{64,96},{80,112},{96,0},{112,16},{1... | collective-permute-start | bytes 1376264 | tf_op jit(solution)/shard_map/ppermute | solution.py:78
  188.2 11.5 %collective-permute-start.10 = (bf16[256,896]{1,0:T(8,128)(2,1)S(1)}, bf16[256,896]{1,0:T(8,128)(2,1)S(1)}, u32[]{:S(2)}, u32[]{:S(2)}) collective-permute-start(bf16[256,896]{1,0:T(8,128)(2,1)S(1)} %get-tuple-element.10), channel_id=1, source_target_pairs={{0,96},{16,112},{32,0},{48,16},{64,32},{80,48},{96,64},{112,80},{1... | collective-permute-start | bytes 1376264 | tf_op jit(solution)/shard_map/ppermute | solution.py:78
  199.8 10.7 %collective-permute-start.8 = (bf16[256,896]{1,0:T(8,128)(2,1)S(1)}, bf16[256,896]{1,0:T(8,128)(2,1)S(1)}, u32[]{:S(2)}, u32[]{:S(2)}) collective-permute-start(bf16[256,896]{1,0:T(8,128)(2,1)S(1)} %collective-permute-done.7), channel_id=1, source_target_pairs={{0,32},{16,48},{32,64},{48,80},{64,96},{80,112},{96,0},{112,16},{1... | collective-permute-start | bytes 1376264 | tf_op jit(solution)/shard_map/ppermute | solution.py:78
  199.8 10.7 %collective-permute-start.11 = (bf16[256,896]{1,0:T(8,128)(2,1)S(1)}, bf16[256,896]{1,0:T(8,128)(2,1)S(1)}, u32[]{:S(2)}, u32[]{:S(2)}) collective-permute-start(bf16[256,896]{1,0:T(8,128)(2,1)S(1)} %collective-permute-done.10), channel_id=1, source_target_pairs={{0,96},{16,112},{32,0},{48,16},{64,32},{80,48},{96,64},{112,80},{1... | collective-permute-start | bytes 1376264 | tf_op jit(solution)/shard_map/ppermute | solution.py:78
  210.5 9.7 %collective-permute-start.9 = (bf16[256,896]{1,0:T(8,128)(2,1)S(1)}, bf16[256,896]{1,0:T(8,128)(2,1)S(1)}, u32[]{:S(2)}, u32[]{:S(2)}) collective-permute-start(bf16[256,896]{1,0:T(8,128)(2,1)S(1)} %collective-permute-done.8), channel_id=1, source_target_pairs={{0,32},{16,48},{32,64},{48,80},{64,96},{80,112},{96,0},{112,16},{1... | collective-permute-start | bytes 1376264 | tf_op jit(solution)/shard_map/ppermute | solution.py:78
  210.5 9.7 %collective-permute-start.12 = (bf16[256,896]{1,0:T(8,128)(2,1)S(1)}, bf16[256,896]{1,0:T(8,128)(2,1)S(1)}, u32[]{:S(2)}, u32[]{:S(2)}) collective-permute-start(bf16[256,896]{1,0:T(8,128)(2,1)S(1)} %collective-permute-done.11), channel_id=1, source_target_pairs={{0,96},{16,112},{32,0},{48,16},{64,32},{80,48},{96,64},{112,80},{1... | collective-permute-start | bytes 1376264 | tf_op jit(solution)/shard_map/ppermute | solution.py:78
  220.3 2.1 copy-start.7
  220.3 2.1 copy-start.2
  222.3 6.8 %collective-permute-start.13 = (bf16[1024,1792]{1,0:T(8,128)(2,1)}, bf16[1024,1792]{1,0:T(8,128)(2,1)}, u32[]{:S(2)}, u32[]{:S(2)}) collective-permute-start(bf16[1024,1792]{1,0:T(8,128)(2,1)} %bitcast.23), channel_id=1, source_target_pairs={{0,16},{16,0},{32,48},{48,32},{64,80},{80,64},{96,112},{112,96},{1... | collective-permute-start | bytes 11010056 | tf_op jit(solution)/shard_map/ppermute | solution.py:85
  225.7 6.4 %copy-start.8 = (bf16[1792,1024]{1,0:T(8,128)(2,1)S(1)}, bf16[1792,1024]{1,0:T(8,128)(2,1)}, u32[]{:S(2)}) copy-start(bf16[1792,1024]{1,0:T(8,128)(2,1)} %param.13) | copy-start | bytes 11010052
Sparse Core Ops, SparseCore 0:
  9.5 54.0 all-gather.1
  242.8 84.8 reduce-scatter.1
where the time goes:
time: 337 us; the launch traced here: 336 us
  waiting for transfers between devices  174 us (52%)
  blocking collectives  37.1 us (11%)
  matrix products  36.1 us (11%)
  local copies, waits for them, and re-layouts  31.7 us (9%)
  other arithmetic  23.2 us (7%)
  starting transfers between devices  20.6 us (6%)
  between operations  13.7 us (4%)
    ppermute x6, waiting for transfers between devices, row_reduce_scatter(): lax.ppermute(acc.astype(jnp.bfloat16), 'row', row_perm(n_row, direction))  54.7 us
    reduce_scatter x1, waiting for transfers between devices, on_device(): lax.psum_scatter(terms[:, :split], 'col', scatter_dimension=0, tiled=True)  47.7 us
    all_to_all x1, blocking collectives, on_device(): right = lax.all_to_all(right, 'col', 0, 0, tiled=False)  37.1 us
    all_gather x1, waiting for transfers between devices, on_device(): gathered = lax.all_gather(tokens, 'col', axis=0, tiled=True)  34.3 us
    ppermute x6, waiting for transfers between devices, row_all_gather(): held = lax.ppermute(held, 'row', row_perm(n_row, direction))  21.1 us
    dot_general x1, matrix products, row_reduce_scatter(): jnp.dot(keep, weights, preferred_element_type=jnp.float32)  14.5 us
    unnamed x20, local copies, waits for them, and re-layouts  13.9 us
    dot_general x1, matrix products, row_reduce_scatter(): jnp.dot(send, weights, preferred_element_type=jnp.float32)  13.4 us
  transfers between devices with their start and end apart: 16, of which 13 were waited for; matrix products, arithmetic and copies ran while one was open for 11% of the time, Pallas kernels for 0%

commit v1 on v0

--- a/solution.py
+++ b/solution.py
@@ -189,7 +189,12 @@
     )
     both_weights = jnp.concatenate([gate_pruned, up_pruned], axis=1)
     rows = tokens.shape[0] // CHUNKS
-    gathered = lax.all_gather(tokens, "col", axis=0, tiled=True)
+
+    def treat_ratios_in(sheet, in_dim):
+        clean = jnp.concatenate(lax.axis_size("col") * [sheet], in_dim)
+        return lax.all_to_all(clean, "col", split_axis=in_dim, concat_axis=in_dim, tiled=True)
+
+    gathered = treat_ratios_in(tokens, 0)
     gathered = gathered.reshape(n_col, CHUNKS, rows, gathered.shape[1])
     outs = []
     previous = None

time: 337 us -> 365 us (1.083)
  local copies, waits for them, and re-layouts: 31.7 us -> 40.6 us
  starting transfers between devices: 20.6 us -> 28.7 us
  blocking collectives: 37.1 us -> 43 us
  waiting for transfers between devices: 174 us -> 179 us
    all_to_all x0 -> x1, waiting for transfers between devices: none -> 40 us  [treat_ratios_in(): lax.all_to_all(clean, 'col', split_axis=in_dim, concat_axis=in_dim, tiled...]
    all_gather x1 -> x0, waiting for transfers between devices: 34.3 us -> none  [on_device(): gathered = lax.all_gather(tokens, 'col', axis=0, tiled=True)]
    unnamed x20 -> x39, local copies, waits for them, and re-layouts: 13.9 us -> 22.8 us
    all_to_all x0 -> x1, starting transfers between devices: none -> 8.04 us  [treat_ratios_in(): lax.all_to_all(clean, 'col', split_axis=in_dim, concat_axis=in_dim, tiled...]
    all_to_all x1, blocking collectives: 37.1 us -> 43 us  [on_device(): right = lax.all_to_all(right, 'col', 0, 0, tiled=False)]
  transfers between devices with their start and end apart: 16 -> 16, of which waited for: 13 -> 13; matrix products, arithmetic and copies ran while one was open for 11% -> 10% of each run, Pallas kernels for 0% -> 0%
where the time goes in v1:
time: 365 us
  waiting for transfers between devices  179 us (49%)
  blocking collectives  43 us (12%)
  local copies, waits for them, and re-layouts  40.6 us (11%)
  matrix products  36.1 us (10%)
  starting transfers between devices  28.7 us (8%)
  other arithmetic  23.1 us (6%)
  between operations  13.8 us (4%)
    ppermute x6, waiting for transfers between devices, row_reduce_scatter(): lax.ppermute(acc.astype(jnp.bfloat16), 'row', row_perm(n_row, direction))  54.9 us
    reduce_scatter x1, waiting for transfers between devices, on_device(): lax.psum_scatter(terms[:, :split], 'col', scatter_dimension=0, tiled=True)  47.7 us
    all_to_all x1, blocking collectives, on_device(): right = lax.all_to_all(right, 'col', 0, 0, tiled=False)  43 us
    all_to_all x1, waiting for transfers between devices, treat_ratios_in(): lax.all_to_all(clean, 'col', split_axis=in_dim, concat_axis=in_dim, tiled...  40 us
    unnamed x39, local copies, waits for them, and re-layouts  22.8 us
    ppermute x6, waiting for transfers between devices, row_all_gather(): held = lax.ppermute(held, 'row', row_perm(n_row, direction))  21.2 us
    dot_general x1, matrix products, row_reduce_scatter(): jnp.dot(keep, weights, preferred_element_type=jnp.float32)  14.5 us
    dot_general x1, matrix products, row_reduce_scatter(): jnp.dot(send, weights, preferred_element_type=jnp.float32)  13.4 us
  transfers between devices with their start and end apart: 16, of which 13 were waited for; matrix products, arithmetic and copies ran while one was open for 10% of the time, Pallas kernels for 0%

profile of v1, /device:TPU:0, one launch (start us, length us, event | category | flops | bytes accessed | tf_op | source)
XLA Modules:
  0.0 364.5 jit_solution(1174572440824380409)
XLA Ops:
  6.5 1.0 constant_dynamic-update-slice_fusion.15
  7.6 1.0 constant_dynamic-update-slice_fusion.14
  8.6 1.0 constant_dynamic-update-slice_fusion.13
  9.5 1.0 constant_dynamic-update-slice_fusion.12
  10.5 1.0 constant_dynamic-update-slice_fusion.11
  11.5 1.0 constant_dynamic-update-slice_fusion.10
  12.4 1.0 constant_dynamic-update-slice_fusion.9
  13.7 1.9 copy-done.3
  15.6 8.0 %all-to-all-start = ((bf16[16,128,1024]{2,1,0:T(8,128)(2,1)}), bf16[16,128,1024]{2,1,0:T(8,128)(2,1)}, u32[]{:S(2)}, u32[]{:S(2)}) async-start(bf16[16,128,1024]{2,1,0:T(8,128)(2,1)} %bitcast.81), calls=%async_computation | async-start | bytes 8388608 | tf_op jit(solution)/shard_map/all_to_all | solution.py:195
  23.7 6.0 %copy.14 = bf16[1024,1792]{0,1:T(8,128)(2,1)} copy(bf16[1024,1792]{1,0:T(8,128)(2,1)} %param.12) | data formatting | bytes 7340032 | tf_op args[2]
  29.7 6.0 %copy.13 = bf16[1024,1792]{0,1:T(8,128)(2,1)} copy(bf16[1024,1792]{1,0:T(8,128)(2,1)} %param.11) | data formatting | bytes 7340032 | tf_op args[1]
  35.8 0.3 fusion.16
  36.2 0.3 fusion.14
  36.6 0.5 broadcast_in_dim.93
  37.1 5.0 %bitcast_select_fusion.1 = bf16[1024,1792]{0,1:T(8,128)(2,1)} fusion(bf16[1024,1792]{0,1:T(8,128)(2,1)} %copy.14, pred[224,8,8,128]{3,2,1,0:T(8,128)(4,1)S(1)} %bitcast.79), kind=kLoop, calls=%fused_computation.5 | loop fusion | flops 1835008 | bytes 9175040 | tf_op jit(solution)/shard_map/jit(_where)/select_n | solution.py:25
  42.1 0.5 broadcast_in_dim.90
  42.7 2.8 bitcast_select_fusion.2
  45.5 40.0 %all-to-all-done = bf16[16,128,1024]{2,1,0:T(8,128)(2,1)} async-done(((bf16[16,128,1024]{2,1,0:T(8,128)(2,1)}), bf16[16,128,1024]{2,1,0:T(8,128)(2,1)}, u32[]{:S(2)}, u32[]{:S(2)}) %all-to-all-start) | async-done | bytes 4194336 | tf_op jit(solution)/shard_map/all_to_all | solution.py:195
  85.5 13.4 %convolution_convert_fusion = bf16[1024,3584]{1,0:T(8,128)(2,1)} fusion(bf16[1024,1792]{0,1:T(8,128)(2,1)} %bitcast_select_fusion.1, bf16[1024,1792]{0,1:T(8,128)(2,1)} %bitcast_select_fusion.2, bf16[2,1024,1024]{2,1,0:T(8,128)(2,1)} %bitcast.1, s32[]{:T(128)S(6)} %select_n.138), kind=kOutput, calls=%fused_computation.1 | convolution fusion | flops 7534542848 | bytes 16777220 | tf_op jit(solution)/shard_map/dot_general | solution.py:44
  98.9 12.0 %collective-permute-done = bf16[1024,3584]{1,0:T(8,128)(2,1)} collective-permute-done((bf16[1024,3584]{1,0:T(8,128)(2,1)}, bf16[1024,3584]{1,0:T(8,128)(2,1)}, u32[]{:S(2)}, u32[]{:S(2)}) %collective-permute-start) | collective-permute-done | bytes 7340064 | tf_op jit(solution)/shard_map/ppermute | solution.py:46
  110.9 14.5 %add_convert_fusion = bf16[1024,3584]{1,0:T(8,128)(2,1)} fusion(bf16[1024,3584]{1,0:T(8,128)(2,1)} %collective-permute-done, bf16[1024,1792]{0,1:T(8,128)(2,1)} %bitcast_select_fusion.1, bf16[1024,1792]{0,1:T(8,128)(2,1)} %bitcast_select_fusion.2, bf16[2,1024,1024]{2,1,0:T(8,128)(2,1)} %bitcast.1, s32[]{:T(128)S(6)} %select_n.135), kind=kOutput, calls=%fused_computation | convolution fusion | flops 7549222912 | bytes 24117252 | tf_op jit(solution)/shard_map/dot_general | solution.py:47
  125.4 5.4 %fusion.22 = (bf16[4,256,1792]{2,1,0:T(8,128)(2,1)S(1)}, bf16[4,256,1792]{2,1,0:T(8,128)(2,1)}) fusion(bf16[4,256,3584]{2,1,0:T(8,128)(2,1)} %bitcast.77), kind=kLoop, calls=%fused_computation.75 | loop fusion | bytes 14680064 | tf_op jit(solution)/shard_map/slice | solution.py:55
  130.8 1.8 copy-done.1
  132.7 1.7 collective-permute-start.1
  134.3 2.2 dynamic-slice_bitcast_fusion
  136.6 1.7 collective-permute-start.4
  138.2 18.2 %collective-permute-done.1 = bf16[256,1792]{1,0:T(8,128)(2,1)S(1)} collective-permute-done((bf16[256,1792]{1,0:T(8,128)(2,1)S(1)}, bf16[256,1792]{1,0:T(8,128)(2,1)S(1)}, u32[]{:S(2)}, u32[]{:S(2)}) %collective-permute-start.1) | collective-permute-done | bytes 917536 | tf_op jit(solution)/shard_map/ppermute | solution.py:59
  156.4 1.4 fusion.9
  157.8 0.4 collective-permute-start.2
  158.2 0.7 collective-permute-done.4
  158.9 2.4 fusion.7
  161.3 3.0 collective-permute-start.5
  164.2 16.5 %collective-permute-done.2 = bf16[256,1792]{1,0:T(8,128)(2,1)S(1)} collective-permute-done((bf16[256,1792]{1,0:T(8,128)(2,1)S(1)}, bf16[256,1792]{1,0:T(8,128)(2,1)S(1)}, u32[]{:S(2)}, u32[]{:S(2)}) %collective-permute-start.2) | collective-permute-done | bytes 917536 | tf_op jit(solution)/shard_map/ppermute | solution.py:59
  180.7 1.4 fusion.8
  182.1 0.1 collective-permute-start.3
  182.2 1.3 collective-permute-done.5
  183.4 2.7 fusion.6
  186.1 3.7 %collective-permute-start.6 = (bf16[256,1792]{1,0:T(8,128)(2,1)}, bf16[256,1792]{1,0:T(8,128)(2,1)S(1)}, u32[]{:S(2)}, u32[]{:S(2)}) collective-permute-start(bf16[256,1792]{1,0:T(8,128)(2,1)} %fusion.6), channel_id=1, source_target_pairs={{0,96},{16,112},{32,0},{48,16},{64,32},{80,48},{96,64},{112,80},{1... | collective-permute-start | bytes 2752520 | tf_op jit(solution)/shard_map/ppermute | solution.py:59
  189.8 14.3 %collective-permute-done.3 = bf16[256,1792]{1,0:T(8,128)(2,1)S(1)} collective-permute-done((bf16[256,1792]{1,0:T(8,128)(2,1)S(1)}, bf16[256,1792]{1,0:T(8,128)(2,1)S(1)}, u32[]{:S(2)}, u32[]{:S(2)}) %collective-permute-start.3) | collective-permute-done | bytes 917536 | tf_op jit(solution)/shard_map/ppermute | solution.py:59
  204.1 4.0 %collective-permute-done.6 = bf16[256,1792]{1,0:T(8,128)(2,1)S(1)} collective-permute-done((bf16[256,1792]{1,0:T(8,128)(2,1)}, bf16[256,1792]{1,0:T(8,128)(2,1)S(1)}, u32[]{:S(2)}, u32[]{:S(2)}) %collective-permute-start.6) | collective-permute-done | bytes 917536 | tf_op jit(solution)/shard_map/ppermute | solution.py:59
  208.1 2.2 fusion.5
  210.3 0.1 fusion.24
  210.4 0.1 collective-permute-start.7
  210.5 3.7 %collective-permute-start.10 = (bf16[256,896]{1,0:T(8,128)(2,1)S(1)}, bf16[256,896]{1,0:T(8,128)(2,1)S(1)}, u32[]{:S(2)}, u32[]{:S(2)}) collective-permute-start(bf16[256,896]{1,0:T(8,128)(2,1)S(1)} %get-tuple-element.10), channel_id=1, source_target_pairs={{0,96},{16,112},{32,0},{48,16},{64,32},{80,48},{96,64},{112,80},{1... | collective-permute-start | bytes 1376264 | tf_op jit(solution)/shard_map/ppermute | solution.py:78
  214.2 0.1 broadcast.73.clone.1
  214.4 0.1 broadcast.73.clone
  214.6 7.6 %collective-permute-done.7 = bf16[256,896]{1,0:T(8,128)(2,1)S(1)} collective-permute-done((bf16[256,896]{1,0:T(8,128)(2,1)S(1)}, bf16[256,896]{1,0:T(8,128)(2,1)S(1)}, u32[]{:S(2)}, u32[]{:S(2)}) %collective-permute-start.7) | collective-permute-done | bytes 458784 | tf_op jit(solution)/shard_map/ppermute | solution.py:78
  222.2 3.2 collective-permute-start.11
  225.5 7.3 %collective-permute-done.8 = bf16[256,896]{1,0:T(8,128)(2,1)S(1)} collective-permute-done((bf16[256,896]{1,0:T(8,128)(2,1)S(1)}, bf16[256,896]{1,0:T(8,128)(2,1)S(1)}, u32[]{:S(2)}, u32[]{:S(2)}) %collective-permute-start.8) | collective-permute-done | bytes 458784 | tf_op jit(solution)/shard_map/ppermute | solution.py:78
  232.8 3.2 collective-permute-start.12
  236.2 6.3 %collective-permute-done.9 = bf16[256,896]{1,0:T(8,128)(2,1)S(1)} collective-permute-done((bf16[256,896]{1,0:T(8,128)(2,1)S(1)}, bf16[256,896]{1,0:T(8,128)(2,1)S(1)}, u32[]{:S(2)}, u32[]{:S(2)}) %collective-permute-start.9) | collective-permute-done | bytes 458784 | tf_op jit(solution)/shard_map/ppermute | solution.py:78
  242.7 2.0 pad_maximum_fusion.3
  244.8 0.3 fusion.12
  245.1 0.5 broadcast_in_dim.89
  245.6 2.5 bitcast_dynamic-update-slice_fusion.1
  248.1 3.4 collective-permute-done.13
  251.5 2.5 bitcast_dynamic-update-slice_fusion
  253.9 0.5 broadcast_in_dim.105
  254.5 8.2 %convolution_convert_fusion.2 = bf16[2048,1024]{1,0:T(8,128)(2,1)S(1)} fusion(bf16[2048,1792]{1,0:T(8,128)(2,1)S(1)} %bitcast.78, bf16[1792,1024]{1,0:T(8,128)(2,1)S(1)} %copy-done.10, pred[224,8,8,128]{3,2,1,0:T(8,128)(4,1)S(1)} %bitcast.82), kind=kOutput, calls=%fused_computation.7 | convolution fusion | flops 7520124928 | bytes 17039360 | tf_op jit(solution)/shard_map/dot_general | solution.py:206
  262.7 2.3 fusion.23
  265.1 43.0 %all_to_all.14 = bf16[16,128,512]{2,1,0:T(8,128)(2,1)S(1)} all-to-all(bf16[16,128,512]{2,1,0:T(8,128)(2,1)} %bitcast.76), channel_id=1, replica_groups=mesh['row'=8,'col'=16] {'col'}, dimensions={0} | all-to-all | bytes 4194304 | tf_op jit(solution)/shard_map/all_to_all | solution.py:216
  308.1 0.3 reduce_sum.12
  308.4 47.7 %reduce-scatter.2.cloned.1.call-done = bf16[128,512]{1,0:T(8,128)(2,1)} async-done(((bf16[2048,512]{1,0:T(8,128)(2,1)}), bf16[128,512]{1,0:T(8,128)(2,1)}) %reduce-scatter.2.cloned.1.call-update) | async-done | bytes 131088 | tf_op jit(solution)/shard_map/reduce_scatter | solution.py:214
  356.0 1.6 pad_maximum_fusion.4
  (52 shorter events, 1.0 us)
Async XLA Ops:
  6.5 6.9 %copy-start = (bf16[128,1024]{1,0:T(8,128)(2,1)S(1)}, bf16[128,1024]{1,0:T(8,128)(2,1)}, u32[]{:S(2)}) copy-start(bf16[128,1024]{1,0:T(8,128)(2,1)} %param.10) | copy-start | bytes 786436
  13.7 2.0 copy-start.3
  15.6 69.9 %all-to-all-start = ((bf16[16,128,1024]{2,1,0:T(8,128)(2,1)}), bf16[16,128,1024]{2,1,0:T(8,128)(2,1)}, u32[]{:S(2)}, u32[]{:S(2)}) async-start(bf16[16,128,1024]{2,1,0:T(8,128)(2,1)} %bitcast.81), calls=%async_computation | async-start | bytes 8388608 | tf_op jit(solution)/shard_map/all_to_all | solution.py:195
  23.7 332.4 %reduce-scatter.2.cloned.1.call-start = ((), (), s32[]{:S(2)}) async-start(), calls=%async_computation.3 | async-start | bytes 2228224 | tf_op jit(solution)/shard_map/reduce_scatter | solution.py:214
  29.7 6.0 %copy-start.7 = (s32[14]{0:T(128)S(1)}, s32[14]{0:T(128)}, u32[]{:S(2)}) copy-start(s32[14]{0:T(128)} %param.17) | copy-start | bytes 172
  29.7 6.1 %copy-start.5 = (s32[14,48]{1,0:T(8,128)S(1)}, s32[14,48]{1,0:T(8,128)}, u32[]{:S(2)}) copy-start(s32[14,48]{1,0:T(8,128)} %param.16) | copy-start | bytes 8068
  29.7 6.1 %copy-start.6 = (s32[14,48]{1,0:T(8,128)S(1)}, s32[14,48]{1,0:T(8,128)}, u32[]{:S(2)}) copy-start(s32[14,48]{1,0:T(8,128)} %param.14) | copy-start | bytes 8068
  29.7 6.4 %copy-start.8 = (s32[14]{0:T(128)S(1)}, s32[14]{0:T(128)}, u32[]{:S(2)}) copy-start(s32[14]{0:T(128)} %param.15) | copy-start | bytes 172
  37.1 5.6 %copy-start.2 = (bf16[1024,1792]{0,1:T(8,128)(2,1)S(1)}, bf16[1024,1792]{0,1:T(8,128)(2,1)}, u32[]{:S(2)}) copy-start(bf16[1024,1792]{0,1:T(8,128)(2,1)} %copy.13) | copy-start | bytes 11010052
  98.9 12.0 %collective-permute-start = (bf16[1024,3584]{1,0:T(8,128)(2,1)}, bf16[1024,3584]{1,0:T(8,128)(2,1)}, u32[]{:S(2)}, u32[]{:S(2)}) collective-permute-start(bf16[1024,3584]{1,0:T(8,128)(2,1)} %convolution_convert_fusion), channel_id=1, source_target_pairs={{0,16},{16,0},{32,48},{48,32},{64,80},{80,64},{96,112},{112,96},{1... | collective-permute-start | bytes 22020104 | tf_op jit(solution)/shard_map/ppermute | solution.py:46
  130.8 1.8 copy-start.1
  132.7 23.7 %collective-permute-start.1 = (bf16[256,1792]{1,0:T(8,128)(2,1)S(1)}, bf16[256,1792]{1,0:T(8,128)(2,1)S(1)}, u32[]{:S(2)}, u32[]{:S(2)}) collective-permute-start(bf16[256,1792]{1,0:T(8,128)(2,1)S(1)} %dynamic-slice_bitcast_fusion.1), channel_id=1, source_target_pairs={{0,32},{16,48},{32,64},{48,80},{64,96},{80,112},{96,0},{112,16},{1... | collective-permute-start | bytes 2752520 | tf_op jit(solution)/shard_map/ppermute | solution.py:59
  136.6 22.3 %collective-permute-start.4 = (bf16[256,1792]{1,0:T(8,128)(2,1)}, bf16[256,1792]{1,0:T(8,128)(2,1)S(1)}, u32[]{:S(2)}, u32[]{:S(2)}) collective-permute-start(bf16[256,1792]{1,0:T(8,128)(2,1)} %dynamic-slice_bitcast_fusion), channel_id=1, source_target_pairs={{0,96},{16,112},{32,0},{48,16},{64,32},{80,48},{96,64},{112,80},{1... | collective-permute-start | bytes 2752520 | tf_op jit(solution)/shard_map/ppermute | solution.py:59
  157.8 22.9 %collective-permute-start.2 = (bf16[256,1792]{1,0:T(8,128)(2,1)S(1)}, bf16[256,1792]{1,0:T(8,128)(2,1)S(1)}, u32[]{:S(2)}, u32[]{:S(2)}) collective-permute-start(bf16[256,1792]{1,0:T(8,128)(2,1)S(1)} %fusion.9), channel_id=1, source_target_pairs={{0,32},{16,48},{32,64},{48,80},{64,96},{80,112},{96,0},{112,16},{1... | collective-permute-start | bytes 2752520 | tf_op jit(solution)/shard_map/ppermute | solution.py:59
  161.3 22.2 %collective-permute-start.5 = (bf16[256,1792]{1,0:T(8,128)(2,1)}, bf16[256,1792]{1,0:T(8,128)(2,1)}, u32[]{:S(2)}, u32[]{:S(2)}) collective-permute-start(bf16[256,1792]{1,0:T(8,128)(2,1)} %fusion.7), channel_id=1, source_target_pairs={{0,96},{16,112},{32,0},{48,16},{64,32},{80,48},{96,64},{112,80},{1... | collective-permute-start | bytes 2752520 | tf_op jit(solution)/shard_map/ppermute | solution.py:59
  182.1 22.0 %collective-permute-start.3 = (bf16[256,1792]{1,0:T(8,128)(2,1)S(1)}, bf16[256,1792]{1,0:T(8,128)(2,1)S(1)}, u32[]{:S(2)}, u32[]{:S(2)}) collective-permute-start(bf16[256,1792]{1,0:T(8,128)(2,1)S(1)} %fusion.8), channel_id=1, source_target_pairs={{0,32},{16,48},{32,64},{48,80},{64,96},{80,112},{96,0},{112,16},{1... | collective-permute-start | bytes 2752520 | tf_op jit(solution)/shard_map/ppermute | solution.py:59
  186.1 22.0 %collective-permute-start.6 = (bf16[256,1792]{1,0:T(8,128)(2,1)}, bf16[256,1792]{1,0:T(8,128)(2,1)S(1)}, u32[]{:S(2)}, u32[]{:S(2)}) collective-permute-start(bf16[256,1792]{1,0:T(8,128)(2,1)} %fusion.6), channel_id=1, source_target_pairs={{0,96},{16,112},{32,0},{48,16},{64,32},{80,48},{96,64},{112,80},{1... | collective-permute-start | bytes 2752520 | tf_op jit(solution)/shard_map/ppermute | solution.py:59
  210.4 11.7 %collective-permute-start.7 = (bf16[256,896]{1,0:T(8,128)(2,1)S(1)}, bf16[256,896]{1,0:T(8,128)(2,1)S(1)}, u32[]{:S(2)}, u32[]{:S(2)}) collective-permute-start(bf16[256,896]{1,0:T(8,128)(2,1)S(1)} %get-tuple-element.9), channel_id=1, source_target_pairs={{0,32},{16,48},{32,64},{48,80},{64,96},{80,112},{96,0},{112,16},{1... | collective-permute-start | bytes 1376264 | tf_op jit(solution)/shard_map/ppermute | solution.py:78
  210.5 11.7 %collective-permute-start.10 = (bf16[256,896]{1,0:T(8,128)(2,1)S(1)}, bf16[256,896]{1,0:T(8,128)(2,1)S(1)}, u32[]{:S(2)}, u32[]{:S(2)}) collective-permute-start(bf16[256,896]{1,0:T(8,128)(2,1)S(1)} %get-tuple-element.10), channel_id=1, source_target_pairs={{0,96},{16,112},{32,0},{48,16},{64,32},{80,48},{96,64},{112,80},{1... | collective-permute-start | bytes 1376264 | tf_op jit(solution)/shard_map/ppermute | solution.py:78
  222.2 10.7 %collective-permute-start.8 = (bf16[256,896]{1,0:T(8,128)(2,1)S(1)}, bf16[256,896]{1,0:T(8,128)(2,1)S(1)}, u32[]{:S(2)}, u32[]{:S(2)}) collective-permute-start(bf16[256,896]{1,0:T(8,128)(2,1)S(1)} %collective-permute-done.7), channel_id=1, source_target_pairs={{0,32},{16,48},{32,64},{48,80},{64,96},{80,112},{96,0},{112,16},{1... | collective-permute-start | bytes 1376264 | tf_op jit(solution)/shard_map/ppermute | solution.py:78
  222.2 10.7 %collective-permute-start.11 = (bf16[256,896]{1,0:T(8,128)(2,1)S(1)}, bf16[256,896]{1,0:T(8,128)(2,1)S(1)}, u32[]{:S(2)}, u32[]{:S(2)}) collective-permute-start(bf16[256,896]{1,0:T(8,128)(2,1)S(1)} %collective-permute-done.10), channel_id=1, source_target_pairs={{0,96},{16,112},{32,0},{48,16},{64,32},{80,48},{96,64},{112,80},{1... | collective-permute-start | bytes 1376264 | tf_op jit(solution)/shard_map/ppermute | solution.py:78
  232.8 9.7 %collective-permute-start.9 = (bf16[256,896]{1,0:T(8,128)(2,1)S(1)}, bf16[256,896]{1,0:T(8,128)(2,1)S(1)}, u32[]{:S(2)}, u32[]{:S(2)}) collective-permute-start(bf16[256,896]{1,0:T(8,128)(2,1)S(1)} %collective-permute-done.8), channel_id=1, source_target_pairs={{0,32},{16,48},{32,64},{48,80},{64,96},{80,112},{96,0},{112,16},{1... | collective-permute-start | bytes 1376264 | tf_op jit(solution)/shard_map/ppermute | solution.py:78
  232.8 9.7 %collective-permute-start.12 = (bf16[256,896]{1,0:T(8,128)(2,1)S(1)}, bf16[256,896]{1,0:T(8,128)(2,1)S(1)}, u32[]{:S(2)}, u32[]{:S(2)}) collective-permute-start(bf16[256,896]{1,0:T(8,128)(2,1)S(1)} %collective-permute-done.11), channel_id=1, source_target_pairs={{0,96},{16,112},{32,0},{48,16},{64,32},{80,48},{96,64},{112,80},{1... | collective-permute-start | bytes 1376264 | tf_op jit(solution)/shard_map/ppermute | solution.py:78
  242.7 2.1 copy-start.9
  242.7 2.1 copy-start.4
  244.7 6.8 %collective-permute-start.13 = (bf16[1024,1792]{1,0:T(8,128)(2,1)}, bf16[1024,1792]{1,0:T(8,128)(2,1)}, u32[]{:S(2)}, u32[]{:S(2)}) collective-permute-start(bf16[1024,1792]{1,0:T(8,128)(2,1)} %bitcast.24), channel_id=1, source_target_pairs={{0,16},{16,0},{32,48},{48,32},{64,80},{80,64},{96,112},{112,96},{1... | collective-permute-start | bytes 11010056 | tf_op jit(solution)/shard_map/ppermute | solution.py:85
  248.1 6.4 %copy-start.10 = (bf16[1792,1024]{1,0:T(8,128)(2,1)S(1)}, bf16[1792,1024]{1,0:T(8,128)(2,1)}, u32[]{:S(2)}) copy-start(bf16[1792,1024]{1,0:T(8,128)(2,1)} %param.13) | copy-start | bytes 11010052
Sparse Core Ops, SparseCore 0:
  265.2 90.8 reduce-scatter.1
